TPU v7x, 32 devices: a whole 2x2x4 slice. The times are simulated.
32 devices in a mesh: leaf: 2 (over core), prow: 2 (over x), pcol: 8 (over z, y).
Axes of the slice: x: 2, y: 2, z: 4, core: 2. Of those that a mesh axis runs over, the one named last changes fastest.
Arguments:
- known_above: bfloat16 [2, 2, 256, 256], P('prow'), may hold values from -6 to 6
- seed_top: float32 [2, 2, 8, 2, 256, 256], P('leaf', 'prow', 'pcol'), may hold values from -6 to 6
- seed_mid: float32 [2, 2, 8, 2, 256, 256], P('leaf', 'prow', 'pcol'), may hold values from -6 to 6
- seed_low: float32 [2, 2, 8, 2, 256, 256], P('leaf', 'prow', 'pcol'), may hold values from -6 to 6
- inverse_top: bfloat16 [2, 2, 8, 2, 256, 256], P('leaf', 'prow', 'pcol'), may hold values from -0.375 to 0.375
- middle_inverses: bfloat16 [2, 2, 8, 2, 256, 256], P('leaf', 'prow', 'pcol'), may hold values from -0.375 to 0.375
- inverse_low: bfloat16 [2, 2, 8, 2, 256, 256], P('leaf', 'prow', 'pcol'), may hold values from -0.375 to 0.375
- tiles_top: bfloat16 [2, 2, 8, 58, 256, 256], P('leaf', 'prow', 'pcol'), may hold values from -0.046875 to 0.046875
- tiles_mid: bfloat16 [2, 2, 8, 58, 256, 256], P('leaf', 'prow', 'pcol'), may hold values from -0.046875 to 0.046875
- tiles_low: bfloat16 [2, 2, 8, 58, 256, 256], P('leaf', 'prow', 'pcol'), may hold values from -0.046875 to 0.046875
- top_source_rows: int32 [2, 2, 8, 58], P('leaf', 'prow', 'pcol'), may hold values from 0 to 1
- source_mid: int32 [2, 2, 8, 58], P('leaf', 'prow', 'pcol'), may hold values from 0 to 33
- lowest_source_rows: int32 [2, 2, 8, 58], P('leaf', 'prow', 'pcol'), may hold values from 0 to 49
- target_top: int32 [2, 2, 8, 58], P('leaf', 'prow', 'pcol'), may hold values from 0 to 3
- target_mid: int32 [2, 2, 8, 58], P('leaf', 'prow', 'pcol'), may hold values from 0 to 3
- target_low: int32 [2, 2, 8, 58], P('leaf', 'prow', 'pcol'), may hold values from 0 to 3
Outputs:
- solved_top: float32 [2, 2, 8, 2, 256, 256], P('leaf', 'prow', 'pcol')
- solved_mid: float32 [2, 2, 8, 2, 256, 256], P('leaf', 'prow', 'pcol')
- solved_low: float32 [2, 2, 8, 2, 256, 256], P('leaf', 'prow', 'pcol')
All inputs are finite; a program needn't handle non-finite values.
Results may differ from a plain program's by a relative error of at most 0.015.
Values may be sent and summed in bfloat16 or wider, within the bound.
A program may use at most 192 MiB of HBM per device.

v0:
```python
import functools

import jax
import jax.numpy as jnp
from jax import lax
from jax.experimental import pallas as pl
from jax.experimental.pallas import tpu as pltpu
from jax.sharding import PartitionSpec as P

MESH = pl.DeviceIdType.MESH
CHUNKS = 4
HOP = 3.2
SPACING = 3.0
GROUP = 8
PAIR = 2


def kernel(dims, *refs):
    n_leaf, n_prow, n_pcol, n_tiles, per_dev, upper, width, depth = dims
    rows = width // CHUNKS
    columns = n_prow * per_dev
    line = n_pcol // PAIR
    (known, *rest) = refs
    seeds, rest = rest[:3], rest[3:]
    inverses, rest = rest[:3], rest[3:]
    tiles_hbm, rest = rest[:3], rest[3:]
    sources, rest = rest[:3], rest[3:]
    targets, rest = rest[:3], rest[3:]
    outs, rest = rest[:3], rest[3:]
    tiles, rest = rest[:3], rest[3:]
    top_store, rest = rest[:CHUNKS], rest[CHUNKS:]
    mid_store, rest = rest[:CHUNKS], rest[CHUNKS:]
    seg, x_send, x_recv, seed_vm, inv_vm, out_vm = rest[:6]
    tile_sem, in_sem, out_sem, xs_sem, xr_sem, g_send, g_recv = rest[6:]

    leaf = lax.axis_index("leaf")
    prow = lax.axis_index("prow")
    pcol = lax.axis_index("pcol")
    z = pcol // PAIR
    y = pcol % PAIR

    cuts = [0, 16, 32, n_tiles]
    parts = list(zip(cuts[:-1], cuts[1:]))

    def tile_copy(level, part):
        lo, hi = parts[part] if level == 0 else (0, n_tiles)
        return pltpu.make_async_copy(
            tiles_hbm[level].at[pl.ds(lo, hi - lo)],
            tiles[level].at[pl.ds(lo, hi - lo)],
            tile_sem.at[level, part],
        )

    def seed_copy(level):
        return pltpu.make_async_copy(seeds[level], seed_vm.at[level], in_sem.at[0, level])

    def inverse_copy(level):
        return pltpu.make_async_copy(inverses[level], inv_vm.at[level], in_sem.at[1, level])

    def out_copy(level, chunk):
        here = pl.ds(chunk * rows, rows)
        return pltpu.make_async_copy(
            out_vm.at[level, :, here, :], outs[level].at[:, here, :], out_sem.at[level, chunk]
        )

    for part in range(len(parts)):
        tile_copy(0, part).start()
    for level in range(3):
        if level > 0:
            tile_copy(level, 0).start()
        seed_copy(level).start()
        inverse_copy(level).start()

    barrier = pltpu.get_barrier_semaphore()

    def greet(where):
        pl.semaphore_signal(barrier, inc=1, device_id=where, device_id_type=MESH)

    for off in range(1, n_prow):
        greet({"prow": lax.rem(prow + off, n_prow)})
    for off in range(1, n_leaf):
        greet({"leaf": lax.rem(leaf + off, n_leaf)})
    greet({"pcol": z * PAIR + (1 - y)})

    @pl.when(z > 0)
    def _():
        greet({"pcol": pcol - PAIR})

    @pl.when(z < line - 1)
    def _():
        greet({"pcol": pcol + PAIR})

    for chunk in range(CHUNKS):
        top_store[chunk][0:upper] = known[:, chunk * rows : (chunk + 1) * rows, :]
    seg[n_tiles] = jnp.zeros((rows, depth), jnp.float32)

    near = (z > 0).astype(jnp.int32) + (z < line - 1).astype(jnp.int32)
    pl.semaphore_wait(barrier, (n_prow - 1) + (n_leaf - 1) + 1 + near)

    def row_block(level, chunk, source):
        if level == 0:
            return known[source, chunk * rows : (chunk + 1) * rows, :]
        if level == 1:
            return top_store[chunk][source]
        count = upper + n_leaf * n_pcol * per_dev
        first = top_store[chunk][jnp.minimum(source, count - 1)]
        second = mid_store[chunk][jnp.maximum(source - count, 0)]
        return lax.select(source < count, first, second)

    def products(level, chunk):
        def step(t, last):
            source = sources[level][t]
            target = targets[level][t]
            product = jnp.dot(
                row_block(level, chunk, source), tiles[level][t], preferred_element_type=jnp.float32
            )
            before = last[0]
            for m in range(1, columns):
                before = jnp.where(target == m, last[m], before)
            seg[t] = seg[before] + product
            return tuple(jnp.where(target == m, t, last[m]) for m in range(columns))

        def group(i, last):
            for j in range(GROUP):
                last = step(i * GROUP + j, last)
            return last

        last = tuple(jnp.int32(n_tiles) for _ in range(columns))
        if chunk == 0 and level > 0:
            tile_copy(level, 0).wait()
        spans = parts if level == 0 and chunk == 0 else [(0, n_tiles)]
        for part, (lo, hi) in enumerate(spans):
            if level == 0 and chunk == 0:
                tile_copy(0, part).wait()
            last = lax.fori_loop(lo // GROUP, hi // GROUP, group, last)
            for t in range(hi // GROUP * GROUP, hi):
                last = step(jnp.int32(t), last)

        def partial(q, d):
            where = last[d]
            for other in range(1, n_prow):
                where = jnp.where(q == other, last[other * per_dev + d], where)
            return seg[where].astype(jnp.bfloat16)

        for off in range(1, n_prow):
            q = lax.rem(prow + off, n_prow)
            for d in range(per_dev):
                x_send[level, chunk, off, d] = partial(q, d)
            x_copy(level, chunk, off).start()
        for d in range(per_dev):
            x_send[level, chunk, 0, d] = partial(prow, d)

    def x_copy(level, chunk, off):
        return pltpu.make_async_remote_copy(
            src_ref=x_send.at[level, chunk, off],
            dst_ref=x_recv.at[level, chunk, off - 1],
            send_sem=xs_sem.at[level, chunk, off - 1],
            recv_sem=xr_sem.at[level, chunk, off - 1],
            device_id={"prow": lax.rem(prow + off, n_prow)},
            device_id_type=MESH,
        )

    def piece(g, chunk, l, c):
        if g == 0:
            return top_store[chunk].at[pl.ds(upper + (l * n_pcol + c) * per_dev, per_dev)]
        return mid_store[chunk].at[pl.ds(c * per_dev, per_dev)]

    def solve(level, chunk):
        for off in range(1, n_prow):
            x_copy(level, chunk, off).wait_recv()
        here = slice(chunk * rows, (chunk + 1) * rows)
        if chunk == 0:
            seed_copy(level).wait()
            inverse_copy(level).wait()
        for d in range(per_dev):
            sums = x_send[level, chunk, 0, d].astype(jnp.float32)
            for off in range(1, n_prow):
                sums = sums + x_recv[level, chunk, off - 1, d].astype(jnp.float32)
            reduced = (seed_vm[level, d, here, :] - sums).astype(jnp.bfloat16)
            solved = lax.dot_general(
                reduced,
                inv_vm[level, d],
                (((1,), (1,)), ((), ())),
                preferred_element_type=jnp.float32,
            )
            out_vm[level, d, here, :] = solved
            if level == 0:
                top_store[chunk][upper + (leaf * n_pcol + pcol) * per_dev + d] = solved.astype(
                    jnp.bfloat16
                )
            elif level == 1:
                mid_store[chunk][pcol * per_dev + d] = solved.astype(jnp.bfloat16)

        out_copy(level, chunk).start()

    UP, DOWN, ACROSS, SIBLING = 0, 1, 2, 3

    def copy(g, chunk, way, c, l=None):
        where = {
            UP: {"pcol": pcol + PAIR},
            DOWN: {"pcol": pcol - PAIR},
            ACROSS: {"pcol": z * PAIR + (1 - y)},
            SIBLING: {"leaf": 1 - leaf},
        }[way]
        l = leaf if l is None else l
        return pltpu.make_async_remote_copy(
            src_ref=piece(g, chunk, l, c),
            dst_ref=piece(g, chunk, l, c),
            send_sem=g_send.at[g, chunk, way, c],
            recv_sem=g_recv.at[g, chunk, l, c],
            device_id=where,
            device_id_type=MESH,
        )

    def arrived(g, chunk, c, l=None):
        copy(g, chunk, SIBLING, c, l).wait_recv()

    def hand_on(g, chunk, o, same, act):
        c = o * PAIR + (y if same else 1 - y)
        may_turn = chunk % 2 == 1
        turned = (o == 0) | (o == line - 1)

        def when(condition, way):
            @pl.when(condition)
            def _():
                act(copy(g, chunk, way, c))

        up = (z < line - 1) & (o <= z)
        down = (z > 0) & (o >= z)
        if same:
            when(up, UP)
            when(down, DOWN)
            if may_turn:
                when((o == z) | jnp.logical_not(turned), ACROSS)
            else:
                act(copy(g, chunk, ACROSS, c))
        elif may_turn:
            when(turned & up, UP)
            when(turned & down, DOWN)
        if g == 0:
            act(copy(g, chunk, SIBLING, c))

    def start(dma):
        dma.start()

    def wait_send(dma):
        dma.wait_send()

    def launch(g, chunk):
        hand_on(g, chunk, z, True, start)

    def take(g, chunk, o, same):
        arrived(g, chunk, o * PAIR + (y if same else 1 - y))
        hand_on(g, chunk, o, same, start)

    def take_at(g, chunk, s, same):
        @pl.when(z >= s)
        def _():
            take(g, chunk, z - s, same)

        @pl.when(z + s < line)
        def _():
            take(g, chunk, z + s, same)

    def step_gather(g, chunk, s):
        if s < line:
            take_at(g, chunk, s, True)
        if s == 1:
            take(g, chunk, z, False)
        else:
            take_at(g, chunk, s - 1, False)

    def finish(g, chunk):
        if g == 0:
            for c in range(n_pcol):
                arrived(g, chunk, c, 1 - leaf)

    events = []

    def at(time, act, *which):
        events.append((time, len(events), act, which))

    free = 0.0
    solved_at = [5.0 + 1.5 * chunk for chunk in range(CHUNKS)]
    for chunk in range(CHUNKS):
        at(0.0, products, 0, chunk)
    for g in range(2):
        for chunk in range(CHUNKS):
            begin = max(solved_at[chunk] + 0.1, free)
            free = begin + SPACING
            at(solved_at[chunk], solve, g, chunk)
            at(begin, launch, g, chunk)
            for s in range(1, line + 1):
                at(begin + s * HOP, step_gather, g, chunk, s)
            done = begin + (line + 0.4) * HOP
            at(done, finish, g, chunk)
            at(done, products, g + 1, chunk)
            solved_at[chunk] = done + 4.0
    for chunk in range(CHUNKS):
        at(solved_at[chunk], solve, 2, chunk)
    for _, _, act, which in sorted(events, key=lambda e: e[:2]):
        act(*which)

    for level in range(3):
        for chunk in range(CHUNKS):
            out_copy(level, chunk).wait()
            for off in range(1, n_prow):
                x_copy(level, chunk, off).wait_send()
    for g in range(2):
        for chunk in range(CHUNKS):

            def left(o, carry):
                hand_on(g, chunk, o, True, wait_send)
                hand_on(g, chunk, o, False, wait_send)
                return carry

            lax.fori_loop(0, line, left, 0)


def settle(*refs):
    sources, outs, held, sem = refs[:3], refs[3:6], refs[6], refs[7]

    def taken(i):
        return pltpu.make_async_copy(sources[i], held.at[i], sem.at[0, i])

    def given(i):
        return pltpu.make_async_copy(held.at[i], outs[i], sem.at[1, i])

    for i in range(3):
        taken(i).start()
    for i in range(3):
        taken(i).wait()
        given(i).start()
    for i in range(3):
        given(i).wait()


def local(*args):
    n_leaf, n_prow, n_pcol = (lax.axis_size(a) for a in ("leaf", "prow", "pcol"))
    known = args[0][0]
    seeds = [a[0, 0, 0] for a in args[1:4]]
    inverses = [a[0, 0, 0] for a in args[4:7]]
    tiles = [a[0, 0, 0] for a in args[7:10]]
    sources = [a[0, 0, 0] for a in args[10:13]]
    targets = [a[0, 0, 0] for a in args[13:16]]
    upper, width, depth = known.shape
    n_tiles = tiles[0].shape[0]
    per_dev = seeds[0].shape[0]
    rows = width // CHUNKS
    vmem = pl.BlockSpec(memory_space=pltpu.VMEM)
    smem = pl.BlockSpec(memory_space=pltpu.SMEM)
    hbm = pl.BlockSpec(memory_space=pl.ANY)
    bf16, f32 = jnp.bfloat16, jnp.float32
    dims = (n_leaf, n_prow, n_pcol, n_tiles, per_dev, upper, width, depth)
    outs = pl.pallas_call(
        functools.partial(kernel, dims),
        out_shape=[jax.ShapeDtypeStruct((per_dev, width, depth), f32)] * 3,
        in_specs=[vmem] + [hbm] * 9 + [smem] * 6,
        out_specs=[hbm] * 3,
        scratch_shapes=[pltpu.VMEM((n_tiles, depth, depth), bf16)] * 3
        + [pltpu.VMEM((upper + n_leaf * n_pcol * per_dev, rows, depth), bf16)] * CHUNKS
        + [pltpu.VMEM((n_pcol * per_dev, rows, depth), bf16)] * CHUNKS
        + [
            pltpu.VMEM((n_tiles + 1, rows, depth), f32),
            pltpu.VMEM((3, CHUNKS, n_prow, per_dev, rows, depth), bf16),
            pltpu.VMEM((3, CHUNKS, n_prow - 1, per_dev, rows, depth), bf16),
            pltpu.VMEM((3, per_dev, width, depth), f32),
            pltpu.VMEM((3, per_dev, depth, depth), bf16),
            pltpu.VMEM((3, per_dev, width, depth), f32),
            pltpu.SemaphoreType.DMA((3, 3)),
            pltpu.SemaphoreType.DMA((2, 3)),
            pltpu.SemaphoreType.DMA((3, CHUNKS)),
            pltpu.SemaphoreType.DMA((3, CHUNKS, n_prow - 1)),
            pltpu.SemaphoreType.DMA((3, CHUNKS, n_prow - 1)),
            pltpu.SemaphoreType.DMA((2, CHUNKS, 4, n_pcol)),
            pltpu.SemaphoreType.DMA((2, CHUNKS, n_leaf, n_pcol)),
        ],
        compiler_params=pltpu.CompilerParams(
            collective_id=0, has_side_effects=True, vmem_limit_bytes=67043328
        ),
        name="window",
    )(known, *seeds, *inverses, *tiles, *sources, *targets)
    outs = pl.pallas_call(
        settle,
        out_shape=[jax.ShapeDtypeStruct((per_dev, width, depth), f32)] * 3,
        in_specs=[hbm] * 3,
        out_specs=[hbm] * 3,
        scratch_shapes=[
            pltpu.VMEM((3, per_dev, width, depth), f32),
            pltpu.SemaphoreType.DMA((2, 3)),
        ],
        name="settle",
    )(*outs)
    return tuple(o[None, None, None] for o in outs)


def solution(mesh):
    blocks = P("leaf", "prow", "pcol", None, None, None)
    lists = P("leaf", "prow", "pcol", None)
    in_specs = (P("prow", None, None, None),) + (blocks,) * 9 + (lists,) * 6
    return jax.shard_map(
        local, mesh=mesh, in_specs=in_specs, out_specs=(blocks,) * 3, check_vma=False
    )
```

profile of v0, /device:TPU:0, one launch (start us, length us, event | category | flops | bytes accessed | tf_op | source)
XLA Modules:
  0.0 82.7 jit_solution(7933067920347844648)
XLA Ops:
  0.6 79.8 %window.1 = (f32[2,256,256]{2,1,0:T(8,128)}, f32[2,256,256]{2,1,0:T(8,128)}, f32[2,256,256]{2,1,0:T(8,128)}) custom-call(bf16[2,256,256]{2,1,0:T(8,128)(2,1)} %bitcast.25, f32[2,256,256]{2,1,0:T(8,128)} %bitcast.22, f32[2,256,256]{2,1,0:T(8,128)} %bitcast.23, f32[2,256,256]{2,1,0:T(8,128)} %bitcast.24, bf16[2,256,256]{2,1,0:T(8,128)(2,1)} %bitcast.26, ...), custom_call_target="tpu_custom_call" | custom-call | tf_op jit(solution)/shard_map/window/pallas_call | solution.py:354
  80.5 2.2 %settle.1 = (f32[2,256,256]{2,1,0:T(8,128)}, f32[2,256,256]{2,1,0:T(8,128)}, f32[2,256,256]{2,1,0:T(8,128)}) custom-call(f32[2,256,256]{2,1,0:T(8,128)} %get-tuple-element.9.refs_0_, f32[2,256,256]{2,1,0:T(8,128)} %get-tuple-element.10.refs_1_, f32[2,256,256]{2,1,0:T(8,128)} %get-tuple-element.11.refs_2_), custom_call_target="tpu_custom_call" | custom-call | tf_op jit(solution)/shard_map/settle/pallas_call | solution.py:382
where the time goes:
time: 82.9 us; the launch traced here: 82.7 us
  Pallas kernels  82.1 us (99%)
    pallas_call x1, Pallas kernels, local(): pl.pallas_call(functools.partial(kernel, dims), out_shape=[jax.ShapeDtype...  79.8 us
    pallas_call x1, Pallas kernels, local(): pl.pallas_call(settle, out_shape=[jax.ShapeDtypeStruct((per_dev, width, d...  2.23 us

commit v1 on v0

--- a/solution.py
+++ b/solution.py
@@ -11,7 +11,7 @@
 CHUNKS = 4
 HOP = 3.2
 SPACING = 3.0
-GROUP = 8
+GROUP = 29
 PAIR = 2
 
 
@@ -39,7 +39,7 @@
     z = pcol // PAIR
     y = pcol % PAIR
 
-    cuts = [0, 16, 32, n_tiles]
+    cuts = [0, *range(GROUP, n_tiles, GROUP), n_tiles]
     parts = list(zip(cuts[:-1], cuts[1:]))
 
     def tile_copy(level, part):
@@ -366,7 +366,7 @@
             pltpu.VMEM((3, per_dev, width, depth), f32),
             pltpu.VMEM((3, per_dev, depth, depth), bf16),
             pltpu.VMEM((3, per_dev, width, depth), f32),
-            pltpu.SemaphoreType.DMA((3, 3)),
+            pltpu.SemaphoreType.DMA((3, pl.cdiv(n_tiles, GROUP))),
             pltpu.SemaphoreType.DMA((2, 3)),
             pltpu.SemaphoreType.DMA((3, CHUNKS)),
             pltpu.SemaphoreType.DMA((3, CHUNKS, n_prow - 1)),

time: 82.9 us -> 75.8 us (0.914)
  Pallas kernels: 82.1 us -> 75 us
    pallas_call x1, Pallas kernels: 79.8 us -> 72.7 us  [local(): pl.pallas_call(functools.partial(kernel, dims), out_shape=[jax.ShapeDtype...]
where the time goes in v1:
time: 75.8 us; the launch traced here: 75.6 us
  Pallas kernels  75 us (99%)
    pallas_call x1, Pallas kernels, local(): pl.pallas_call(functools.partial(kernel, dims), out_shape=[jax.ShapeDtype...  72.7 us
    pallas_call x1, Pallas kernels, local(): pl.pallas_call(settle, out_shape=[jax.ShapeDtypeStruct((per_dev, width, d...  2.23 us

profile of v1, /device:TPU:0, one launch (start us, length us, event | category | flops | bytes accessed | tf_op | source)
XLA Modules:
  0.0 75.6 jit_solution(9371558325677498688)
XLA Ops:
  0.6 72.7 %window.1 = (f32[2,256,256]{2,1,0:T(8,128)}, f32[2,256,256]{2,1,0:T(8,128)}, f32[2,256,256]{2,1,0:T(8,128)}) custom-call(bf16[2,256,256]{2,1,0:T(8,128)(2,1)} %bitcast.25, f32[2,256,256]{2,1,0:T(8,128)} %bitcast.22, f32[2,256,256]{2,1,0:T(8,128)} %bitcast.23, f32[2,256,256]{2,1,0:T(8,128)} %bitcast.24, bf16[2,256,256]{2,1,0:T(8,128)(2,1)} %bitcast.26, ...), custom_call_target="tpu_custom_call" | custom-call | tf_op jit(solution)/shard_map/window/pallas_call | solution.py:354
  73.4 2.2 %settle.1 = (f32[2,256,256]{2,1,0:T(8,128)}, f32[2,256,256]{2,1,0:T(8,128)}, f32[2,256,256]{2,1,0:T(8,128)}) custom-call(f32[2,256,256]{2,1,0:T(8,128)} %get-tuple-element.9.refs_0_, f32[2,256,256]{2,1,0:T(8,128)} %get-tuple-element.10.refs_1_, f32[2,256,256]{2,1,0:T(8,128)} %get-tuple-element.11.refs_2_), custom_call_target="tpu_custom_call" | custom-call | tf_op jit(solution)/shard_map/settle/pallas_call | solution.py:382
